TPU v7x, 256 devices: a whole 4x4x8 slice. The times are simulated.
256 devices in a mesh: segment: 16 (over y_lo, x, core), ctx: 16 (over y_hi, z).
Axes of the slice: x: 4, y: 4 (y_hi: 2, y_lo: 2; y = y_hi * 2 + y_lo), z: 8, core: 2. Of those that a mesh axis runs over, the one named last changes fastest.
Arguments:
- carried_down: bfloat16 [16, 2048, 1408], P('segment', 'ctx'), may hold values from -6 to 6
- carried_up: bfloat16 [16, 2048, 1408], P('segment', 'ctx'), may hold values from -6 to 6
- skip_bank: bfloat16 [16, 3, 2048, 1408], P('segment', None, 'ctx'), may hold values from -6 to 6
- queue: bfloat16 [8, 2048, 1408], P(None, 'ctx'), may hold values from -6 to 6
- next_entry: int32 [8], replicated, may hold values from 0 to 7, each once
- skip_slot: int32 [2, 16], P(None, 'segment'), may hold values from 0 to 2
- w_qkv: bfloat16 [16, 3, 1408, 1408], P('segment', None, 'ctx'), may hold values from -1.6523056 to 1.6523056
- w_out: bfloat16 [16, 1408, 1408], P('segment', 'ctx'), may hold values from -0.5 to 0.5
- w_skip: bfloat16 [16, 2816, 1408], P('segment', 'ctx'), may hold values from -0.109375 to 0.109375
- gains: float32 [16, 2, 1408], P('segment'), may hold values from 0.1 to 1.9
Outputs:
- desc_out: bfloat16 [2, 16, 2048, 1408], P(None, 'segment', 'ctx')
- asc_out: bfloat16 [2, 16, 2048, 1408], P(None, 'segment', 'ctx')
All inputs are finite; a program needn't handle non-finite values.
Results may differ from a plain program's by a relative error of at most 0.015.
Values may be sent and summed in bfloat16 or wider, within the bound.
A program may use at most 128 MiB of HBM per device.

v0:
```python
import jax
import jax.numpy as jnp
from jax import lax
from jax.sharding import PartitionSpec as P

HEAD = 88
D = 1408


def from_behind(value, axis, steps):
    count = lax.axis_size(axis)
    leading, last = (max(0, -steps), min(count, count - steps))
    return lax.ppermute(value, axis, [(source, source + steps) for source in range(leading, last)])


def layer_norm(values, gain):
    center = values - jnp.mean(values, axis=-1, keepdims=True)
    spread = jnp.mean(center * center, axis=-1, keepdims=True)
    return center * lax.rsqrt(spread + 1e-06) * gain


def attend(stacked):
    queries, keys, values = (stacked[0], stacked[1], stacked[2])
    local_heads, width, length = queries.shape
    block = 512
    blocks = length // block
    grouped = queries.reshape(local_heads, width, blocks, block).transpose(2, 0, 1, 3)

    def one_block(query_block):
        scores = jnp.einsum(
            "hen,hem->hnm", query_block, keys, preferred_element_type=jnp.float32
        ) * HEAD ** (-0.5)
        peak = jnp.max(scores, axis=2, keepdims=True)
        powers = jnp.exp(scores - peak)
        totals = jnp.sum(powers, axis=2)
        mixed = jnp.einsum(
            "hem,hnm->hen", values, powers.astype(jnp.bfloat16), preferred_element_type=jnp.float32
        )
        return (mixed / totals[:, None, :]).astype(jnp.bfloat16)

    results = lax.map(one_block, grouped)
    return results.transpose(1, 2, 0, 3).reshape(local_heads, width, length)


def send_down(descended):
    return from_behind(descended, "segment", 1)


def send_up(ascended):
    return from_behind(ascended, "segment", -1)


def on_device(
    carried_down, carried_up, skip_bank, queue, next_entry, skip_slot, w_qkv, w_out, w_skip, gains
):
    segment_count = lax.axis_size("segment")
    place = lax.axis_index("segment")
    tok_rows = carried_down.shape[1]
    local_heads = w_qkv.shape[2] // HEAD
    full_out, full_skip = (
        lax.all_gather(w_out[0], "ctx", axis=0, tiled=True),
        lax.all_gather(w_skip[0], "ctx", axis=0, tiled=True),
    )
    own_qkv = w_qkv[0].reshape(3, local_heads, HEAD, D)

    def descend(inputs):
        normed = layer_norm(inputs.astype(jnp.float32), gains[0, 0]).astype(jnp.bfloat16)
        made = jnp.einsum(
            "khed,td->khet",
            own_qkv,
            lax.all_gather(normed, "ctx", axis=0, tiled=True),
            preferred_element_type=jnp.float32,
        )
        projected = made.astype(jnp.bfloat16)
        head_out = attend(projected)
        returned = lax.all_to_all(head_out, "ctx", split_axis=2, concat_axis=0, tiled=True)
        merged = returned.reshape(D, tok_rows)
        added = jnp.einsum("ft,fd->td", merged, full_out, preferred_element_type=jnp.float32)
        return (inputs.astype(jnp.float32) + added).astype(jnp.bfloat16)

    def ascend(rising, slot):
        skip = lax.dynamic_index_in_dim(skip_bank[0], slot, 0, keepdims=False)
        joined = jnp.concatenate([rising, skip], axis=1)
        projected = jnp.dot(joined, full_skip, preferred_element_type=jnp.float32)
        return layer_norm(projected, gains[0, 1]).astype(jnp.bfloat16)

    first_down = descend(carried_down[0])
    first_up = ascend(carried_up[0], skip_slot[0, 0])
    arrive_down = send_down(first_down)
    arrive_up = send_up(first_up)
    entering = lax.dynamic_index_in_dim(queue, next_entry[0], 0, keepdims=False)
    down_next = jnp.where(place == 0, entering, arrive_down)
    up_next = jnp.where(place == segment_count - 1, first_down, arrive_up)
    second_down = descend(down_next)
    second_up = ascend(up_next, skip_slot[1, 0])
    desc_out = jnp.stack([first_down, second_down])[:, None]
    asc_out = jnp.stack([first_up, second_up])[:, None]
    return (desc_out, asc_out)


def solution(mesh):
    in_specs = (
        P("segment", "ctx", None),
        P("segment", "ctx", None),
        P("segment", None, "ctx", None),
        P(None, "ctx", None),
        P(),
        P(None, "segment"),
        P("segment", None, "ctx", None),
        P("segment", "ctx", None),
        P("segment", "ctx", None),
        P("segment", None, None),
    )
    out_specs = (P(None, "segment", "ctx", None), P(None, "segment", "ctx", None))
    return jax.shard_map(
        on_device, mesh=mesh, in_specs=in_specs, out_specs=out_specs, check_vma=False
    )
```

profile of v0, /device:TPU:32, one launch (start us, length us, event | category | flops | bytes accessed | tf_op | source)
XLA Modules:
  0.0 543.4 jit_solution(12254006201471091412)
XLA Ops:
  8.0 1.1 convert_reduce_fusion.1
  9.2 1.2 fusion.95
  10.4 2.0 fusion.97
  13.9 1.3 fusion.109
  18.8 1.9 dynamic-slice_bitcast_fusion.1
  20.7 105.0 %all-gather.7.cloned.1.call-done = bf16[2048,1408]{1,0:T(8,128)(2,1)} async-done(((bf16[128,1408]{1,0:T(8,128)(2,1)}), bf16[2048,1408]{1,0:T(8,128)(2,1)}) %all-gather.7.cloned.1.call-update) | async-done | bytes 5767184 | tf_op jit(solution)/shard_map/all_gather | solution.py:71
  125.7 4.5 fusion.73
  130.3 10.5 %while.20 = (s32[]{:T(128)}, bf16[4,1,88,512]{3,2,1,0:T(8,128)(2,1)S(1)}, bf16[4,1,88,512]{3,2,1,0:T(8,128)(2,1)S(1)}, bf16[1,88,2048]{2,1,0:T(8,128)(2,1)S(1)}, bf16[1,88,2048]{2,1,0:T(8,128)(2,1)S(1)}, /*index=5*/s32[]{:T(128)}) while((s32[]{:T(128)}, bf16[4,1,88,512]{3,2,1,0:T(8,128)(2,1)S(1)}, bf16[4,1,88,512]{3,2,1,0:T(8,128)(2,1)S(1)}, ...), condition=%wide.region_5.6_spmd, body=%wide.region_2.5_spmd.sunk | while | flops 377576448 | bytes 13494349 | solution.py:41
  141.9 11.5 %reduce.13 = bf16[2048,88]{1,0:T(8,128)(2,1)S(1)} reduce(bf16[2048,1,88]{2,1,0:T(2,128)(2,1)S(1)} %bitcast.194, bf16[]{:T(256)} %broadcast.140), dimensions={1}, to_apply=%bitcast.149.reduce_sub_computation | reduce | bytes 720898
  153.5 1.9 reshape.170
  155.4 5.2 all-to-all-start
  160.8 100.3 %all-gather.13.cloned.1.call-done = bf16[1,2816,1408]{2,1,0:T(8,128)(2,1)} async-done(((bf16[1,176,1408]{2,1,0:T(8,128)(2,1)}), bf16[1,2816,1408]{2,1,0:T(8,128)(2,1)}) %all-gather.13.cloned.1.call-update) | async-done | bytes 7929872 | tf_op jit(solution)/shard_map/all_gather | solution.py:62
  261.1 4.7 fusion.110
  266.9 1.3 collective-permute-start.1
  268.2 2.1 reshape.171
  271.2 89.2 %all-gather.11.cloned.1.call-done = bf16[1,1408,1408]{2,1,0:T(8,128)(2,1)} async-done(((bf16[1,88,1408]{2,1,0:T(8,128)(2,1)}), bf16[1,1408,1408]{2,1,0:T(8,128)(2,1)}) %all-gather.11.cloned.1.call-update) | async-done | bytes 3964944 | tf_op jit(solution)/shard_map/all_gather | solution.py:61
  360.4 3.1 broadcast_select_fusion
  363.5 1.3 collective-permute-start
  364.9 1.1 collective-permute-done
  366.1 1.2 convert_reduce_fusion
  367.5 1.0 fusion.94
  369.5 4.7 fusion.111
  375.2 106.9 %all-gather.9.cloned.1.call-done = bf16[2048,1408]{1,0:T(8,128)(2,1)} async-done(((bf16[128,1408]{1,0:T(8,128)(2,1)}), bf16[2048,1408]{1,0:T(8,128)(2,1)}) %all-gather.9.cloned.1.call-update) | async-done | bytes 5767184 | tf_op jit(solution)/shard_map/all_gather | solution.py:71
  482.1 4.5 fusion.70
  486.8 10.7 %while.21 = (s32[]{:T(128)}, bf16[4,1,88,512]{3,2,1,0:T(8,128)(2,1)S(1)}, bf16[4,1,88,512]{3,2,1,0:T(8,128)(2,1)S(1)}, bf16[1,88,2048]{2,1,0:T(8,128)(2,1)S(1)}, bf16[1,88,2048]{2,1,0:T(8,128)(2,1)S(1)}, /*index=5*/s32[]{:T(128)}) while((s32[]{:T(128)}, bf16[4,1,88,512]{3,2,1,0:T(8,128)(2,1)S(1)}, bf16[4,1,88,512]{3,2,1,0:T(8,128)(2,1)S(1)}, ...), condition=%wide.region_11.12_spmd, body=%wide.region_8.11_spmd.sunk | while | flops 377576448 | bytes 13494349 | solution.py:41
  498.1 11.5 %reduce.14 = bf16[2048,88]{1,0:T(8,128)(2,1)S(1)} reduce(bf16[2048,1,88]{2,1,0:T(2,128)(2,1)S(1)} %bitcast.195, bf16[]{:T(256)} %broadcast.140), dimensions={1}, to_apply=%bitcast.151.reduce_sub_computation | reduce | bytes 720898
  509.6 1.9 reshape.172
  511.5 5.2 all-to-all-start.1
  516.8 11.6 %all-to-all-done.1 = bf16[16,2,5632]{2,1,0:T(2,128)(2,1)} async-done(((bf16[16,2,5632]{2,1,0:T(2,128)(2,1)}), bf16[16,2,5632]{2,1,0:T(2,128)(2,1)}, u32[]{:S(2)}, u32[]{:S(2)}) %all-to-all-start.1) | async-done | bytes 360480 | tf_op jit(solution)/shard_map/all_to_all | solution.py:76
  528.4 3.4 reshape.173
  532.7 2.9 fusion.82
  535.6 1.3 maximum_bitcast_fusion
  (88 shorter events, 30.5 us)
Async XLA Ops:
  7.2 118.5 %copy-start = (bf16[1,3,88,1408]{3,2,1,0:T(8,128)(2,1)S(1)}, bf16[1,3,88,1408]{3,2,1,0:T(8,128)(2,1)}, u32[]{:S(2)}) copy-start(bf16[1,3,88,1408]{3,2,1,0:T(8,128)(2,1)} %param.20) | copy-start | bytes 2230276
  7.2 118.5 %all-gather.7.cloned.1.call-start = ((), (), s32[]{:S(2)}) async-start(), calls=%async_computation.2 | async-start | bytes 6127616 | tf_op jit(solution)/shard_map/all_gather | solution.py:71
  12.4 248.7 %all-gather.13.cloned.1.call-start = ((), (), s32[]{:S(2)}) async-start(), calls=%async_computation.5 | async-start | bytes 8425472 | tf_op jit(solution)/shard_map/all_gather | solution.py:62
  13.2 347.2 %all-gather.11.cloned.1.call-start = ((), (), s32[]{:S(2)}) async-start(), calls=%async_computation.4 | async-start | bytes 4212736 | tf_op jit(solution)/shard_map/all_gather | solution.py:61
  140.8 120.3 %copy-start.9 = (bf16[1,128,1408]{2,1,0:T(8,128)(2,1)S(1)}, bf16[1,128,1408]{2,1,0:T(8,128)(2,1)}, u32[]{:S(2)}) copy-start(bf16[1,128,1408]{2,1,0:T(8,128)(2,1)} %param.15) | copy-start | bytes 1081348
  155.4 112.9 %all-to-all-start = ((bf16[16,2,5632]{2,1,0:T(2,128)(2,1)}), bf16[16,2,5632]{2,1,0:T(2,128)(2,1)S(1)}, u32[]{:S(2)}, u32[]{:S(2)}) async-start(bf16[16,2,5632]{2,1,0:T(2,128)(2,1)} %reshape.170), calls=%async_computation | async-start | bytes 720896 | tf_op jit(solution)/shard_map/all_to_all | solution.py:76
  160.6 321.6 %all-gather.9.cloned.1.call-start = ((), (), s32[]{:S(2)}) async-start(), calls=%async_computation.3 | async-start | bytes 6127616 | tf_op jit(solution)/shard_map/all_gather | solution.py:71
  265.8 94.6 %copy-start.1 = (bf16[1,128,1408]{2,1,0:T(8,128)(2,1)S(1)}, bf16[1,128,1408]{2,1,0:T(8,128)(2,1)}, u32[]{:S(2)}) copy-start(bf16[1,128,1408]{2,1,0:T(8,128)(2,1)} %param.14) | copy-start | bytes 1081348
  266.9 93.4 %collective-permute-start.1 = (bf16[128,1408]{1,0:T(8,128)(2,1)}, bf16[128,1408]{1,0:T(8,128)(2,1)}, u32[]{:S(2)}, u32[]{:S(2)}) collective-permute-start(bf16[128,1408]{1,0:T(8,128)(2,1)} %multiply_convert_fusion.1), channel_id=1, source_target_pairs={{16,0},{32,16},{48,32},{64,48},{80,64},{96,80},{112,96},{128,112},... | collective-permute-start | bytes 1081352 | tf_op jit(solution)/shard_map/ppermute | solution.py:13
  271.0 93.8 %copy-start.8 = (s32[8]{0:T(128)S(1)}, s32[8]{0:T(128)}, u32[]{:S(2)}) copy-start(s32[8]{0:T(128)} %param.18) | copy-start | bytes 100
  360.4 9.1 %copy-start.7 = (bf16[128,1408]{1,0:T(8,128)(2,1)S(1)}, bf16[128,1408]{1,0:T(8,128)(2,1)}, u32[]{:S(2)}) copy-start(bf16[128,1408]{1,0:T(8,128)(2,1)} %get-tuple-element.95) | copy-start | bytes 1081348
  363.5 10.6 %copy-start.5 = (bf16[128,1408]{1,0:T(8,128)(2,1)}, bf16[128,1408]{1,0:T(8,128)(2,1)S(1)}, u32[]{:S(2)}) copy-start(bf16[128,1408]{1,0:T(8,128)(2,1)S(1)} %get-tuple-element.107) | copy-start | bytes 1081348
  363.5 2.6 collective-permute-start
  374.1 0.9 copy-start.2
  497.5 19.1 %copy-start.3 = (f32[128,1408]{1,0:T(8,128)S(1)}, f32[128,1408]{1,0:T(8,128)}, u32[]{:S(2)}) copy-start(f32[128,1408]{1,0:T(8,128)} %copy-done.2) | copy-start | bytes 2162692
  511.5 17.0 %all-to-all-start.1 = ((bf16[16,2,5632]{2,1,0:T(2,128)(2,1)}), bf16[16,2,5632]{2,1,0:T(2,128)(2,1)}, u32[]{:S(2)}, u32[]{:S(2)}) async-start(bf16[16,2,5632]{2,1,0:T(2,128)(2,1)} %reshape.172), calls=%async_computation.1 | async-start | bytes 720896 | tf_op jit(solution)/shard_map/all_to_all | solution.py:76
  531.8 3.8 copy-start.4
  532.4 3.2 copy-start.6
Sparse Core Ops, SparseCore 0:
  12.5 113.0 all-gather.6
  128.3 132.7 all-gather.12
  263.8 96.5 all-gather.10
  368.7 113.4 all-gather.8
where the time goes:
time: 544 us; the launch traced here: 543 us
  waiting for transfers between devices  416 us (76%)
  other arithmetic  40.2 us (7%)
  matrix products  38.6 us (7%)
  between operations  17.9 us (3%)
  local copies, waits for them, and re-layouts  17.5 us (3%)
  starting transfers between devices  13.3 us (2%)
    all_gather x2, waiting for transfers between devices, descend(): lax.all_gather(normed, 'ctx', axis=0, tiled=True)  212 us
    all_gather x1, waiting for transfers between devices, on_device(): lax.all_gather(w_skip[0], 'ctx', axis=0, tiled=True)  100 us
    all_gather x1, waiting for transfers between devices, on_device(): lax.all_gather(w_out[0], 'ctx', axis=0, tiled=True)  89.2 us
    unnamed x3, other arithmetic  24.3 us
    all_to_all x2, waiting for transfers between devices, descend(): lax.all_to_all(head_out, 'ctx', split_axis=2, concat_axis=0, tiled=True)  11.6 us
  transfers between devices with their start and end apart: 8, of which 6 were waited for; matrix products, arithmetic and copies ran while one was open for 9% of the time, Pallas kernels for 0%

commit v1 on v0

--- a/solution.py
+++ b/solution.py
@@ -5,6 +5,13 @@
 
 HEAD = 88
 D = 1408
+
+
+def all_by_exchange(shard, mesh_axis, d):
+    devices = lax.axis_size(mesh_axis)
+    pieces = jnp.stack([shard for _ in range(devices)])
+    pieces = lax.all_to_all(pieces, mesh_axis, split_axis=0, concat_axis=0)
+    return jnp.concatenate(pieces, axis=d)
 
 
 def from_behind(value, axis, steps):
@@ -68,7 +75,7 @@
         made = jnp.einsum(
             "khed,td->khet",
             own_qkv,
-            lax.all_gather(normed, "ctx", axis=0, tiled=True),
+            all_by_exchange(normed, "ctx", 0),
             preferred_element_type=jnp.float32,
         )
         projected = made.astype(jnp.bfloat16)

time: 544 us -> 564 us (1.037); the launches traced: 543 us -> 557 us
  starting transfers between devices: 13.3 us -> 43.8 us
  waiting for transfers between devices: 416 us -> 396 us
    all_to_all x0 -> x2, waiting for transfers between devices: none -> 270 us  [all_by_exchange(): pieces = lax.all_to_all(pieces, mesh_axis, split_axis=0, concat_axis=0)]
    all_gather x2 -> x0, waiting for transfers between devices: 212 us -> none  [descend(): lax.all_gather(normed, 'ctx', axis=0, tiled=True)]
    all_gather x1, waiting for transfers between devices: 100 us -> 22.9 us  [on_device(): lax.all_gather(w_skip[0], 'ctx', axis=0, tiled=True)]
    all_to_all x0 -> x2, starting transfers between devices: none -> 16.6 us  [all_by_exchange(): pieces = lax.all_to_all(pieces, mesh_axis, split_axis=0, concat_axis=0)]
    all_to_all x2, starting transfers between devices: 10.4 us -> 24.5 us  [descend(): lax.all_to_all(head_out, 'ctx', split_axis=2, concat_axis=0, tiled=True)]
    another operation x2 -> x4, local copies, waits for them, and re-layouts: 0.05 us -> 6.15 us  [the longest x2 6.1 us: all_by_exchange(): pieces = jnp.stack([shard for _ in range(devices)])]
  transfers between devices with their start and end apart: 8 -> 8, of which waited for: 6 -> 6; matrix products, arithmetic and copies ran while one was open for 9% -> 10% of each run, Pallas kernels for 0% -> 0%
where the time goes in v1:
time: 564 us; the launch traced here: 557 us
  waiting for transfers between devices  396 us (70%)
  starting transfers between devices  43.8 us (8%)
  other arithmetic  38.7 us (7%)
  matrix products  38.5 us (7%)
  local copies, waits for them, and re-layouts  21.9 us (4%)
  between operations  18.4 us (3%)
    all_to_all x2, waiting for transfers between devices, all_by_exchange(): pieces = lax.all_to_all(pieces, mesh_axis, split_axis=0, concat_axis=0)  270 us
    all_gather x1, waiting for transfers between devices, on_device(): lax.all_gather(w_out[0], 'ctx', axis=0, tiled=True)  87 us
    all_to_all x2, starting transfers between devices, descend(): lax.all_to_all(head_out, 'ctx', split_axis=2, concat_axis=0, tiled=True)  24.5 us
    unnamed x3, other arithmetic  24.3 us
    all_gather x1, waiting for transfers between devices, on_device(): lax.all_gather(w_skip[0], 'ctx', axis=0, tiled=True)  22.9 us
    all_to_all x2, starting transfers between devices, all_by_exchange(): pieces = lax.all_to_all(pieces, mesh_axis, split_axis=0, concat_axis=0)  16.6 us
    all_to_all x2, waiting for transfers between devices, descend(): lax.all_to_all(head_out, 'ctx', split_axis=2, concat_axis=0, tiled=True)  13.9 us
  transfers between devices with their start and end apart: 8, of which 6 were waited for; matrix products, arithmetic and copies ran while one was open for 10% of the time, Pallas kernels for 0%

profile of v1, /device:TPU:32, one launch (start us, length us, event | category | flops | bytes accessed | tf_op | source)
XLA Modules:
  0.0 557.3 jit_solution(10299314911701261868)
XLA Ops:
  9.9 1.2 fusion.80
  11.1 1.2 fusion.91
  12.3 3.0 stack.19
  15.4 11.3 %all-to-all-start = ((bf16[16,128,1408]{2,1,0:T(8,128)(2,1)}), bf16[16,128,1408]{2,1,0:T(8,128)(2,1)}, u32[]{:S(2)}, u32[]{:S(2)}) async-start(bf16[16,128,1408]{2,1,0:T(8,128)(2,1)} %stack.19), calls=%async_computation | async-start | bytes 11534336 | tf_op jit(solution)/shard_map/all_to_all | solution.py:13
  32.8 148.1 %all-to-all-done = bf16[16,128,1408]{2,1,0:T(8,128)(2,1)} async-done(((bf16[16,128,1408]{2,1,0:T(8,128)(2,1)}), bf16[16,128,1408]{2,1,0:T(8,128)(2,1)}, u32[]{:S(2)}, u32[]{:S(2)}) %all-to-all-start) | async-done | bytes 5767200 | tf_op jit(solution)/shard_map/all_to_all | solution.py:13
  180.9 4.5 fusion.60
  185.6 10.5 %while.20 = (s32[]{:T(128)}, bf16[4,1,88,512]{3,2,1,0:T(8,128)(2,1)S(1)}, bf16[4,1,88,512]{3,2,1,0:T(8,128)(2,1)S(1)}, bf16[1,88,2048]{2,1,0:T(8,128)(2,1)S(1)}, bf16[1,88,2048]{2,1,0:T(8,128)(2,1)S(1)}, /*index=5*/s32[]{:T(128)}) while((s32[]{:T(128)}, bf16[4,1,88,512]{3,2,1,0:T(8,128)(2,1)S(1)}, bf16[4,1,88,512]{3,2,1,0:T(8,128)(2,1)S(1)}, ...), condition=%wide.region_5.6_spmd, body=%wide.region_2.5_spmd.sunk | while | flops 377576448 | bytes 13494349 | solution.py:48
  197.2 11.5 %reduce.13 = bf16[2048,88]{1,0:T(8,128)(2,1)S(1)} reduce(bf16[2048,1,88]{2,1,0:T(2,128)(2,1)S(1)} %bitcast.184, bf16[]{:T(256)} %broadcast.153), dimensions={1}, to_apply=%bitcast.137.reduce_sub_computation | reduce | bytes 720898
  208.7 1.9 reshape.201
  210.6 13.5 %all-to-all-start.1 = ((bf16[16,2,5632]{2,1,0:T(2,128)(2,1)}), bf16[16,2,5632]{2,1,0:T(2,128)(2,1)S(1)}, u32[]{:S(2)}, u32[]{:S(2)}) async-start(bf16[16,2,5632]{2,1,0:T(2,128)(2,1)} %reshape.201), calls=%async_computation.1 | async-start | bytes 720896 | tf_op jit(solution)/shard_map/all_to_all | solution.py:83
  224.1 22.9 %all-gather.7.cloned.1.call-done = bf16[1,2816,1408]{2,1,0:T(8,128)(2,1)} async-done(((bf16[1,176,1408]{2,1,0:T(8,128)(2,1)}), bf16[1,2816,1408]{2,1,0:T(8,128)(2,1)}) %all-gather.7.cloned.1.call-update) | async-done | bytes 7929872 | tf_op jit(solution)/shard_map/all_gather | solution.py:69
  247.1 4.7 fusion.97
  252.9 1.3 collective-permute-start.1
  254.2 2.1 reshape.202
  257.1 87.0 %all-gather.5.cloned.1.call-done = bf16[1,1408,1408]{2,1,0:T(8,128)(2,1)} async-done(((bf16[1,88,1408]{2,1,0:T(8,128)(2,1)}), bf16[1,1408,1408]{2,1,0:T(8,128)(2,1)}) %all-gather.5.cloned.1.call-update) | async-done | bytes 3964944 | tf_op jit(solution)/shard_map/all_gather | solution.py:68
  344.1 3.0 broadcast_select_fusion
  347.2 1.3 collective-permute-start
  348.6 1.1 collective-permute-done
  349.8 1.2 convert_reduce_fusion
  351.5 3.0 stack.21
  354.5 5.2 all-to-all-start.2
  360.7 4.7 fusion.98
  366.4 121.4 %all-to-all-done.2 = bf16[16,128,1408]{2,1,0:T(8,128)(2,1)} async-done(((bf16[16,128,1408]{2,1,0:T(8,128)(2,1)}), bf16[16,128,1408]{2,1,0:T(8,128)(2,1)}, u32[]{:S(2)}, u32[]{:S(2)}) %all-to-all-start.2) | async-done | bytes 5767200 | tf_op jit(solution)/shard_map/all_to_all | solution.py:13
  487.8 4.5 fusion.61
  492.5 10.5 %while.21 = (s32[]{:T(128)}, bf16[4,1,88,512]{3,2,1,0:T(8,128)(2,1)S(1)}, bf16[4,1,88,512]{3,2,1,0:T(8,128)(2,1)S(1)}, bf16[1,88,2048]{2,1,0:T(8,128)(2,1)S(1)}, bf16[1,88,2048]{2,1,0:T(8,128)(2,1)S(1)}, /*index=5*/s32[]{:T(128)}) while((s32[]{:T(128)}, bf16[4,1,88,512]{3,2,1,0:T(8,128)(2,1)S(1)}, bf16[4,1,88,512]{3,2,1,0:T(8,128)(2,1)S(1)}, ...), condition=%wide.region_11.12_spmd, body=%wide.region_8.11_spmd.sunk | while | flops 377576448 | bytes 13494349 | solution.py:48
  503.5 11.5 %reduce.14 = bf16[2048,88]{1,0:T(8,128)(2,1)S(1)} reduce(bf16[2048,1,88]{2,1,0:T(2,128)(2,1)S(1)} %bitcast.185, bf16[]{:T(256)} %broadcast.153), dimensions={1}, to_apply=%bitcast.139.reduce_sub_computation | reduce | bytes 720898
  515.1 1.9 reshape.203
  516.9 11.0 %all-to-all-start.3 = ((bf16[16,2,5632]{2,1,0:T(2,128)(2,1)}), bf16[16,2,5632]{2,1,0:T(2,128)(2,1)}, u32[]{:S(2)}, u32[]{:S(2)}) async-start(bf16[16,2,5632]{2,1,0:T(2,128)(2,1)} %reshape.203), calls=%async_computation.3 | async-start | bytes 720896 | tf_op jit(solution)/shard_map/all_to_all | solution.py:83
  528.1 13.9 %all-to-all-done.3 = bf16[16,2,5632]{2,1,0:T(2,128)(2,1)} async-done(((bf16[16,2,5632]{2,1,0:T(2,128)(2,1)}), bf16[16,2,5632]{2,1,0:T(2,128)(2,1)}, u32[]{:S(2)}, u32[]{:S(2)}) %all-to-all-start.3) | async-done | bytes 360480 | tf_op jit(solution)/shard_map/all_to_all | solution.py:83
  542.0 3.4 reshape.204
  546.3 2.9 fusion.68
  549.2 1.3 maximum_bitcast_fusion
  (92 shorter events, 33.0 us)
Async XLA Ops:
  7.2 173.8 %copy-start = (bf16[1,3,88,1408]{3,2,1,0:T(8,128)(2,1)S(1)}, bf16[1,3,88,1408]{3,2,1,0:T(8,128)(2,1)}, u32[]{:S(2)}) copy-start(bf16[1,3,88,1408]{3,2,1,0:T(8,128)(2,1)} %param.20) | copy-start | bytes 2230276
  7.2 239.9 %all-gather.7.cloned.1.call-start = ((), (), s32[]{:S(2)}) async-start(), calls=%async_computation.5 | async-start | bytes 8425472 | tf_op jit(solution)/shard_map/all_gather | solution.py:69
  15.4 12.1 %copy-start.9 = (s32[2,1]{0,1:T(1,128)S(1)}, s32[2,1]{0,1:T(1,128)}, u32[]{:S(2)}) copy-start(s32[2,1]{0,1:T(1,128)} %param.19) | copy-start | bytes 28
  15.4 16.6 %copy-start.7 = (bf16[1,3,128,1408]{3,2,1,0:T(8,128)(2,1)S(1)}, bf16[1,3,128,1408]{3,2,1,0:T(8,128)(2,1)}, u32[]{:S(2)}) copy-start(bf16[1,3,128,1408]{3,2,1,0:T(8,128)(2,1)} %param.16) | copy-start | bytes 3244036
  15.4 165.5 %all-to-all-start = ((bf16[16,128,1408]{2,1,0:T(8,128)(2,1)}), bf16[16,128,1408]{2,1,0:T(8,128)(2,1)}, u32[]{:S(2)}, u32[]{:S(2)}) async-start(bf16[16,128,1408]{2,1,0:T(8,128)(2,1)} %stack.19), calls=%async_computation | async-start | bytes 11534336 | tf_op jit(solution)/shard_map/all_to_all | solution.py:13
  26.8 317.4 %all-gather.5.cloned.1.call-start = ((), (), s32[]{:S(2)}) async-start(), calls=%async_computation.4 | async-start | bytes 4212736 | tf_op jit(solution)/shard_map/all_gather | solution.py:68
  196.1 51.0 %copy-start.11 = (bf16[1,128,1408]{2,1,0:T(8,128)(2,1)S(1)}, bf16[1,128,1408]{2,1,0:T(8,128)(2,1)}, u32[]{:S(2)}) copy-start(bf16[1,128,1408]{2,1,0:T(8,128)(2,1)} %param.15) | copy-start | bytes 1081348
  210.6 43.6 %all-to-all-start.1 = ((bf16[16,2,5632]{2,1,0:T(2,128)(2,1)}), bf16[16,2,5632]{2,1,0:T(2,128)(2,1)S(1)}, u32[]{:S(2)}, u32[]{:S(2)}) async-start(bf16[16,2,5632]{2,1,0:T(2,128)(2,1)} %reshape.201), calls=%async_computation.1 | async-start | bytes 720896 | tf_op jit(solution)/shard_map/all_to_all | solution.py:83
  251.7 92.4 %copy-start.1 = (bf16[1,128,1408]{2,1,0:T(8,128)(2,1)S(1)}, bf16[1,128,1408]{2,1,0:T(8,128)(2,1)}, u32[]{:S(2)}) copy-start(bf16[1,128,1408]{2,1,0:T(8,128)(2,1)} %param.14) | copy-start | bytes 1081348
  252.9 91.2 %collective-permute-start.1 = (bf16[128,1408]{1,0:T(8,128)(2,1)}, bf16[128,1408]{1,0:T(8,128)(2,1)}, u32[]{:S(2)}, u32[]{:S(2)}) collective-permute-start(bf16[128,1408]{1,0:T(8,128)(2,1)} %multiply_convert_fusion.1), channel_id=1, source_target_pairs={{16,0},{32,16},{48,32},{64,48},{80,64},{96,80},{112,96},{128,112},... | collective-permute-start | bytes 1081352 | tf_op jit(solution)/shard_map/ppermute | solution.py:20
  256.9 91.6 %copy-start.10 = (s32[8]{0:T(128)S(1)}, s32[8]{0:T(128)}, u32[]{:S(2)}) copy-start(s32[8]{0:T(128)} %param.18) | copy-start | bytes 100
  347.2 7.4 %copy-start.5 = (bf16[128,1408]{1,0:T(8,128)(2,1)}, bf16[128,1408]{1,0:T(8,128)(2,1)S(1)}, u32[]{:S(2)}) copy-start(bf16[128,1408]{1,0:T(8,128)(2,1)S(1)} %get-tuple-element.107) | copy-start | bytes 1081348
  347.2 2.6 collective-permute-start
  354.5 6.1 %copy-start.8 = (bf16[128,1408]{1,0:T(8,128)(2,1)S(1)}, bf16[128,1408]{1,0:T(8,128)(2,1)}, u32[]{:S(2)}) copy-start(bf16[128,1408]{1,0:T(8,128)(2,1)} %get-tuple-element.95) | copy-start | bytes 1081348
  354.5 133.3 %all-to-all-start.2 = ((bf16[16,128,1408]{2,1,0:T(8,128)(2,1)}), bf16[16,128,1408]{2,1,0:T(8,128)(2,1)}, u32[]{:S(2)}, u32[]{:S(2)}) async-start(bf16[16,128,1408]{2,1,0:T(8,128)(2,1)} %stack.21), calls=%async_computation.2 | async-start | bytes 11534336 | tf_op jit(solution)/shard_map/all_to_all | solution.py:13
  365.3 0.9 copy-start.2
  503.0 25.0 %copy-start.3 = (f32[128,1408]{1,0:T(8,128)S(1)}, f32[128,1408]{1,0:T(8,128)}, u32[]{:S(2)}) copy-start(f32[128,1408]{1,0:T(8,128)} %copy-done.2) | copy-start | bytes 2162692
  516.9 25.1 %all-to-all-start.3 = ((bf16[16,2,5632]{2,1,0:T(2,128)(2,1)}), bf16[16,2,5632]{2,1,0:T(2,128)(2,1)}, u32[]{:S(2)}, u32[]{:S(2)}) async-start(bf16[16,2,5632]{2,1,0:T(2,128)(2,1)} %reshape.203), calls=%async_computation.3 | async-start | bytes 720896 | tf_op jit(solution)/shard_map/all_to_all | solution.py:83
  545.4 3.8 copy-start.4
  546.1 3.2 copy-start.6
Sparse Core Ops, SparseCore 0:
  10.6 236.4 all-gather.6
  249.7 94.3 all-gather.4
